TPU v7x, 32 devices: a whole 2x2x4 slice. The times are simulated.
32 devices in a mesh: parts: 2 (over x), grid: 8 (over z, y), depth: 2 (over core).
Axes of the slice: x: 2, y: 2, z: 4, core: 2. Of those that a mesh axis runs over, the one named last changes fastest.
Arguments:
- gate_input: bfloat16 [1024, 32768], P(('parts', 'depth'), 'grid'), parts along dimension 0, may hold values from -6 to 6
- up_input: bfloat16 [1024, 32768], P(('parts', 'depth'), 'grid'), parts along dimension 0, may hold values from -6 to 6
- code_values: bfloat16 [32768, 8192], P('grid', 'depth'), may hold values from -6 to 6, as said below
- exponents: int32 [1024, 8192], P('grid', 'depth'), may hold values from -10 to -7
- cotangent: bfloat16 [1024, 8192], P(('parts', 'depth'), 'grid'), parts along dimension 0, may hold values from -1.5 to 1.5
Outputs:
- output_rows: bfloat16 [1024, 8192], P(('parts', 'depth'), 'grid'), parts along dimension 0
- grad_gate: bfloat16 [1024, 32768], P(('parts', 'depth'), 'grid'), parts along dimension 0
- grad_up: bfloat16 [1024, 32768], P(('parts', 'depth'), 'grid'), parts along dimension 0
- grad_weight: bfloat16 [65536, 8192], P(('parts', 'grid'), 'depth'), parts along dimension 0
There are 2 independent parts, one for each index of `parts`. A program takes and returns all parts, laid end to end along the dimension named above; an argument that names none is the same for every part. Nothing has to cross between parts.
Inputs may be any that keep to these rules, and one draw needn't show every extreme that they name: `code_values`: every entry is one of the E2M1 values 0, +-0.5, +-1, +-1.5, +-2, +-3, +-4, +-6.
All inputs are finite; a program needn't handle non-finite values.
Results may differ from a plain program's by a relative error of at most 0.0049.
Values may be sent and summed in bfloat16 or wider, within the bound.
A program may use at most 448 MiB of HBM per device.

v0:
```python
import jax
import jax.numpy as jnp
from jax import lax
from jax.sharding import PartitionSpec as P


def shards(gate_input, up_input, code_values, exponents, cotangent):
    local_units = code_values.shape[0]
    scaled = jnp.exp2(exponents.astype(jnp.float32))
    blocks = code_values.astype(jnp.float32).reshape(local_units // 32, 32, -1) * scaled[:, None, :]
    weight_part = blocks.reshape(local_units, -1).astype(jnp.bfloat16)
    weight = lax.all_gather(weight_part, "depth", axis=1, tiled=True)
    gate_float = gate_input.astype(jnp.float32)
    up_float = up_input.astype(jnp.float32)
    sigmoid_gate = jax.nn.sigmoid(gate_float)
    activated = gate_float * sigmoid_gate
    hidden = (activated * up_float).astype(jnp.bfloat16)
    summed = lax.psum_scatter(
        lax.dot_general(
            weight, hidden, (((0,), (1,)), ((), ())), preferred_element_type=jnp.float32
        ),
        "grid",
        scatter_dimension=0,
        tiled=True,
    )
    output_rows = summed.T.astype(jnp.bfloat16)
    cotangent_all = lax.all_gather(cotangent, "grid", axis=1, tiled=True)
    grad_hidden = lax.dot_general(
        cotangent_all, weight, (((1,), (1,)), ((), ())), preferred_element_type=jnp.float32
    )
    slope = sigmoid_gate * (1.0 + gate_float * (1.0 - sigmoid_gate))
    grad_gate = (grad_hidden * up_float * slope).astype(jnp.bfloat16)
    grad_up = (grad_hidden * activated).astype(jnp.bfloat16)
    weight_term = lax.dot_general(
        hidden, cotangent_all, (((0,), (0,)), ((), ())), preferred_element_type=jnp.float32
    )
    grad_weight = lax.psum_scatter(weight_term, "depth", scatter_dimension=1, tiled=True).astype(
        jnp.bfloat16
    )
    return (output_rows, grad_gate, grad_up, grad_weight)


def solution(mesh):
    in_specs = (
        P(("parts", "depth"), "grid"),
        P(("parts", "depth"), "grid"),
        P("grid", "depth"),
        P("grid", "depth"),
        P(("parts", "depth"), "grid"),
    )
    out_specs = (
        P(("parts", "depth"), "grid"),
        P(("parts", "depth"), "grid"),
        P(("parts", "depth"), "grid"),
        P(("parts", "grid"), "depth"),
    )
    return jax.shard_map(shards, mesh=mesh, in_specs=in_specs, out_specs=out_specs, check_vma=False)
```

profile of v0, /device:TPU:0, one launch (start us, length us, event | category | flops | bytes accessed | tf_op | source)
XLA Modules:
  0.0 557.2 jit_solution(14383094031951518844)
XLA Ops:
  7.2 0.0 all-gather.3.cloned.1.call-start
  7.2 1.9 multiply_exponential_fusion
  9.1 23.3 %fusion = bf16[4096,4096]{1,0:T(8,128)(2,1)} fusion(bf16[4096,4096]{1,0:T(8,128)(2,1)} %param.7, f32[128,4096]{1,0:T(8,128)S(1)} %multiply_exponential_fusion), kind=kLoop, calls=%fused_computation.1 | loop fusion | flops 50331648 | bytes 69206016 | tf_op jit(solution)/shard_map/convert_element_type | solution.py:11
  32.3 0.0 all-gather.3.cloned.1.call-update
  32.4 0.0 all-gather.5.cloned.1.call-start
  32.4 0.7 all-gather.5.cloned.1.call-update
  33.1 0.0 reduce-scatter.3.cloned.1.call-start
  33.2 3.3 copy.9
  36.5 4.1 copy.10
  40.5 89.8 %all-gather.3.cloned.1.call-done = bf16[4096,8192]{1,0:T(8,128)(2,1)} async-done(((bf16[4096,4096]{1,0:T(8,128)(2,1)}), bf16[4096,8192]{1,0:T(8,128)(2,1)}) %all-gather.3.cloned.1.call-update) | async-done | bytes 67108880 | tf_op jit(solution)/shard_map/all_gather | solution.py:12
  130.3 30.2 %fusion.11 = f32[8192,256]{1,0:T(8,128)} fusion(bf16[4096,8192]{1,0:T(8,128)(2,1)} %all-gather.3.cloned.1.call-done, bf16[256,4096]{0,1:T(8,128)(2,1)} %copy.10, bf16[256,4096]{0,1:T(8,128)(2,1)S(1)} %copy.9), kind=kOutput, calls=%fused_computation.20 | convolution fusion | flops 17188257792 | bytes 79691776 | tf_op jit(solution)/shard_map/dot_general | solution.py:19
  160.5 0.0 reduce-scatter.3.cloned.1.call-update
  160.5 0.2 reduce-scatter.5.cloned.1.call-start
  160.8 46.3 %all-gather.5.cloned.1.call-done = bf16[256,8192]{1,0:T(8,128)(2,1)} async-done(((bf16[256,1024]{1,0:T(8,128)(2,1)}), bf16[256,8192]{1,0:T(8,128)(2,1)}) %all-gather.5.cloned.1.call-update) | async-done | bytes 4194320 | tf_op jit(solution)/shard_map/all_gather | solution.py:27
  207.1 49.9 %fusion.9 = f32[4096,8192]{1,0:T(8,128)} fusion(bf16[256,8192]{1,0:T(8,128)(2,1)} %all-gather.5.cloned.1.call-done, bf16[256,4096]{0,1:T(8,128)(2,1)} %copy.10, bf16[256,4096]{0,1:T(8,128)(2,1)S(1)} %copy.9), kind=kOutput, calls=%fused_computation.19 | convolution fusion | flops 17188257792 | bytes 142606336 | tf_op jit(solution)/shard_map/dot_general | solution.py:34
  257.0 0.0 reduce-scatter.5.cloned.1.call-update
  257.1 29.7 %multiply_convert_fusion = (bf16[256,4096]{0,1:T(8,128)(2,1)}, bf16[256,4096]{0,1:T(8,128)(2,1)}) fusion(bf16[256,4096]{0,1:T(8,128)(2,1)S(1)} %copy.9, bf16[256,4096]{0,1:T(8,128)(2,1)} %copy.10, bf16[4096,8192]{1,0:T(8,128)(2,1)} %all-gather.3.cloned.1.call-done, bf16[256,8192]{1,0:T(8,128)(2,1)} %all-gather.5.cloned.1.call-done), kind=kOutput, calls=%fused_computation.16 | convolution fusion | flops 17195597824 | bytes 79691776 | tf_op jit(solution)/shard_map/dot_general | solution.py:28
  286.7 0.0 copy-start
  286.7 4.3 copy.13
  291.0 0.0 copy-done
  291.0 2.8 copy.12
  293.9 64.7 %reduce-scatter.3.cloned.1.call-done = f32[1024,256]{1,0:T(8,128)} async-done(((f32[8192,256]{1,0:T(8,128)}), f32[1024,256]{1,0:T(8,128)}) %reduce-scatter.3.cloned.1.call-update) | async-done | bytes 1048592 | tf_op jit(solution)/shard_map/reduce_scatter | solution.py:18
  358.6 1.3 convert_bitcast_fusion
  359.8 1.0 copy.11
  360.8 157.4 %reduce-scatter.5.cloned.1.call-done = f32[4096,4096]{1,0:T(8,128)} async-done(((f32[4096,8192]{1,0:T(8,128)}), f32[4096,4096]{1,0:T(8,128)}) %reduce-scatter.5.cloned.1.call-update) | async-done | bytes 67108880 | tf_op jit(solution)/shard_map/reduce_scatter | solution.py:37
  518.3 32.4 %convert_element_type.43 = bf16[4096,4096]{1,0:T(8,128)(2,1)} convert(f32[4096,4096]{1,0:T(8,128)} %reduce-scatter.5.cloned.1.call-done) | non-fusion elementwise | flops 16777216 | bytes 100663296 | tf_op jit(solution)/shard_map/convert_element_type | solution.py:37
Async XLA Ops:
  7.2 123.2 %all-gather.3.cloned.1.call-start = ((), (), s32[]{:S(2)}) async-start(), calls=%async_computation.2 | async-start | bytes 100663296 | tf_op jit(solution)/shard_map/all_gather | solution.py:12
  32.4 174.7 %all-gather.5.cloned.1.call-start = ((), (), s32[]{:S(2)}) async-start(), calls=%async_computation.4 | async-start | bytes 4718592 | tf_op jit(solution)/shard_map/all_gather | solution.py:27
  33.1 325.4 %reduce-scatter.3.cloned.1.call-start = ((), (), s32[]{:S(2)}) async-start(), calls=%async_computation.3 | async-start | bytes 9437184 | tf_op jit(solution)/shard_map/reduce_scatter | solution.py:18
  160.5 357.7 %reduce-scatter.5.cloned.1.call-start = ((), (), s32[]{:S(2)}) async-start(), calls=%async_computation.5 | async-start | bytes 201326592 | tf_op jit(solution)/shard_map/reduce_scatter | solution.py:37
  286.7 4.3 copy-start
Sparse Core Ops, SparseCore 0:
  32.5 97.7 all-gather.2
  132.5 74.5 all-gather.4
  211.3 147.2 reduce-scatter.2
  360.8 157.4 reduce-scatter.4
where the time goes:
time: 558 us; the launch traced here: 557 us
  waiting for transfers between devices  359 us (64%)
  matrix products  110 us (20%)
  other arithmetic  58.8 us (11%)
  local copies, waits for them, and re-layouts  15.5 us (3%)
  between operations  13.8 us (2%)
    reduce_scatter x1, waiting for transfers between devices, shards(): lax.psum_scatter(weight_term, 'depth', scatter_dimension=1, tiled=True)  157 us
    all_gather x1, waiting for transfers between devices, shards(): weight = lax.all_gather(weight_part, 'depth', axis=1, tiled=True)  89.8 us
    reduce_scatter x1, waiting for transfers between devices, shards(): lax.psum_scatter(lax.dot_general(weight, hidden, (((0,), (1,)), ((), ()))...  64.7 us
    dot_general x1, matrix products, shards(): lax.dot_general(hidden, cotangent_all, (((0,), (0,)), ((), ())), preferre...  49.9 us
    all_gather x1, waiting for transfers between devices, shards(): cotangent_all = lax.all_gather(cotangent, 'grid', axis=1, tiled=True)  46.3 us
    convert_element_type x1, other arithmetic, shards(): lax.psum_scatter(weight_term, 'depth', scatter_dimension=1, tiled=True)  32.4 us
    dot_general x1, matrix products, shards(): lax.dot_general(weight, hidden, (((0,), (1,)), ((), ())), preferred_eleme...  30.2 us
    dot_general x1, matrix products, shards(): lax.dot_general(cotangent_all, weight, (((1,), (1,)), ((), ())), preferre...  29.7 us
  transfers between devices with their start and end apart: 4, of which 4 were waited for; matrix products, arithmetic and copies ran while one was open for 23% of the time, Pallas kernels for 0%

commit v1 on v0

--- a/solution.py
+++ b/solution.py
@@ -1,7 +1,39 @@
+import functools
 import jax
 import jax.numpy as jnp
 from jax import lax
 from jax.sharding import PartitionSpec as P
+
+
+def store_weights_on_mesh(arr, array_dim):
+    raw_out = list(arr.shape[1:])
+    raw_out[array_dim] *= arr.shape[0]
+    return jnp.moveaxis(arr, 0, array_dim).reshape(raw_out)
+
+
+def start_area(point, a_name):
+    w2 = lax.axis_size(a_name)
+    block_out, carry = (w2, lax.axis_index(a_name))
+    x_new, plain = (point[None], 1)
+    while plain < block_out:
+        row_out = range(block_out)
+        f_next = map(lambda num: (num, num ^ plain), row_out)
+        arr_out = list(f_next)
+        e_now = lax.ppermute(x_new, a_name, arr_out)
+        finding = carry & plain == 0
+        big = jnp.where(finding, x_new, e_now)
+        view_out = jnp.where(finding, e_now, x_new)
+        x_new = jnp.concatenate([big, view_out])
+        plain *= 2
+    return x_new
+
+
+def chunk_draft(xs, w_in, in_dim):
+    y2 = start_area(xs, w_in)
+    return store_weights_on_mesh(y2, in_dim)
+
+
+note_the_classes = functools.partial(chunk_draft, w_in="grid", in_dim=1)
 
 
 def shards(gate_input, up_input, code_values, exponents, cotangent):
@@ -24,7 +56,7 @@
         tiled=True,
     )
     output_rows = summed.T.astype(jnp.bfloat16)
-    cotangent_all = lax.all_gather(cotangent, "grid", axis=1, tiled=True)
+    cotangent_all = note_the_classes(cotangent)
     grad_hidden = lax.dot_general(
         cotangent_all, weight, (((1,), (1,)), ((), ())), preferred_element_type=jnp.float32
     )

time: 558 us -> 636 us (1.14)
  waiting for transfers between devices: 359 us -> 430 us
  local copies, waits for them, and re-layouts: 15.5 us -> 2 us
  matrix products: 110 us -> 120 us
  other arithmetic: 58.8 us -> 66.2 us
    ppermute x0 -> x3, waiting for transfers between devices: none -> 217 us  [start_area(): e_now = lax.ppermute(x_new, a_name, arr_out)]
    reduce_scatter x1, waiting for transfers between devices: 64.7 us -> 0.01 us  [shards(): lax.psum_scatter(lax.dot_general(weight, hidden, (((0,), (1,)), ((), ()))...]
    all_gather x1 -> x0, waiting for transfers between devices: 46.3 us -> none  [shards(): cotangent_all = lax.all_gather(cotangent, 'grid', axis=1, tiled=True)]
    reduce_scatter x1, waiting for transfers between devices: 157 us -> 115 us  [shards(): lax.psum_scatter(weight_term, 'depth', scatter_dimension=1, tiled=True)]
    unnamed x7 -> x8, local copies, waits for them, and re-layouts: 15.5 us -> 2 us
    dot_general x1, matrix products: 29.7 us -> 41 us  [shards(): lax.dot_general(cotangent_all, weight, (((1,), (1,)), ((), ())), preferre...]
    all_gather x1, waiting for transfers between devices: 89.8 us -> 97.9 us  [shards(): weight = lax.all_gather(weight_part, 'depth', axis=1, tiled=True)]
  transfers between devices with their start and end apart: 4 -> 6, of which waited for: 4 -> 5; matrix products, arithmetic and copies ran while one was open for 23% -> 16% of each run, Pallas kernels for 0% -> 0%
where the time goes in v1:
time: 636 us
  waiting for transfers between devices  430 us (68%)
  matrix products  120 us (19%)
  other arithmetic  66.2 us (10%)
  between operations  13.8 us (2%)
    ppermute x3, waiting for transfers between devices, start_area(): e_now = lax.ppermute(x_new, a_name, arr_out)  217 us
    reduce_scatter x1, waiting for transfers between devices, shards(): lax.psum_scatter(weight_term, 'depth', scatter_dimension=1, tiled=True)  115 us
    all_gather x1, waiting for transfers between devices, shards(): weight = lax.all_gather(weight_part, 'depth', axis=1, tiled=True)  97.9 us
    dot_general x1, matrix products, shards(): lax.dot_general(hidden, cotangent_all, (((0,), (0,)), ((), ())), preferre...  48.7 us
    dot_general x1, matrix products, shards(): lax.dot_general(cotangent_all, weight, (((1,), (1,)), ((), ())), preferre...  41 us
    convert_element_type x1, other arithmetic, shards(): lax.psum_scatter(weight_term, 'depth', scatter_dimension=1, tiled=True)  32.4 us
    dot_general x1, matrix products, shards(): lax.dot_general(weight, hidden, (((0,), (1,)), ((), ())), preferred_eleme...  30.4 us
    convert_element_type x1, other arithmetic, shards(): weight_part = blocks.reshape(local_units, -1).astype(jnp.bfloat16)  23.3 us
  transfers between devices with their start and end apart: 6, of which 5 were waited for; matrix products, arithmetic and copies ran while one was open for 16% of the time, Pallas kernels for 0%

profile of v1, /device:TPU:0, one launch (start us, length us, event | category | flops | bytes accessed | tf_op | source)
XLA Modules:
  0.0 635.5 jit_solution(11364330595222417558)
XLA Ops:
  7.2 0.0 all-gather.2.cloned.1.call-start
  7.2 1.9 multiply_exponential_fusion
  9.1 23.3 %fusion = bf16[4096,4096]{1,0:T(8,128)(2,1)} fusion(bf16[4096,4096]{1,0:T(8,128)(2,1)} %param.7, f32[128,4096]{1,0:T(8,128)S(1)} %multiply_exponential_fusion), kind=kLoop, calls=%fused_computation.1 | loop fusion | flops 50331648 | bytes 69206016 | tf_op jit(solution)/shard_map/convert_element_type | solution.py:43
  32.3 0.0 copy-start
  32.4 0.0 all-gather.2.cloned.1.call-update
  32.4 0.0 reduce-scatter.3.cloned.1.call-start
  32.4 97.9 %all-gather.2.cloned.1.call-done = bf16[4096,8192]{1,0:T(8,128)(2,1)} async-done(((bf16[4096,4096]{1,0:T(8,128)(2,1)}), bf16[4096,8192]{1,0:T(8,128)(2,1)}) %all-gather.2.cloned.1.call-update) | async-done | bytes 67108880 | tf_op jit(solution)/shard_map/all_gather | solution.py:44
  130.3 0.0 copy-done
  130.3 30.4 %fusion.11 = f32[8192,256]{1,0:T(8,128)} fusion(bf16[4096,8192]{1,0:T(8,128)(2,1)} %all-gather.2.cloned.1.call-done, bf16[256,4096]{1,0:T(8,128)(2,1)S(1)} %copy-done, bf16[256,4096]{1,0:T(8,128)(2,1)} %param.5), kind=kOutput, calls=%fused_computation.28 | convolution fusion | flops 17188257792 | bytes 79691776 | tf_op jit(solution)/shard_map/dot_general | solution.py:51
  160.7 0.0 copy-start.2
  160.7 0.0 reduce-scatter.3.cloned.1.call-update
  160.7 0.2 reduce-scatter.5.cloned.1.call-start
  161.0 0.8 copy-done.2
  161.8 0.2 copy.10
  162.0 1.8 collective-permute-start
  163.8 18.5 %collective-permute-done = bf16[1,256,1024]{1,2,0:T(8,128)(2,1)S(1)} collective-permute-done((bf16[1,256,1024]{1,2,0:T(8,128)(2,1)S(1)}, bf16[1,256,1024]{1,2,0:T(8,128)(2,1)S(1)}, u32[]{:S(2)}, u32[]{:S(2)}) %collective-permute-start) | collective-permute-done | bytes 524320 | tf_op jit(solution)/shard_map/ppermute | solution.py:22
  182.3 0.1 broadcast_select_fusion.5
  182.3 0.1 pad_maximum_fusion.2
  182.4 1.4 collective-permute-start.1
  183.9 72.0 %collective-permute-done.1 = bf16[2,256,1024]{1,2,0:T(8,128)(2,1)} collective-permute-done((bf16[2,256,1024]{1,2,0:T(8,128)(2,1)S(1)}, bf16[2,256,1024]{1,2,0:T(8,128)(2,1)}, u32[]{:S(2)}, u32[]{:S(2)}) %collective-permute-start.1) | collective-permute-done | bytes 1048608 | tf_op jit(solution)/shard_map/ppermute | solution.py:22
  255.8 1.4 broadcast_select_fusion.3
  257.2 1.5 pad_maximum_fusion.1
  258.7 0.0 collective-permute-start.2
  258.7 126.3 %collective-permute-done.2 = bf16[4,256,1024]{1,2,0:T(8,128)(2,1)} collective-permute-done((bf16[4,256,1024]{1,2,0:T(8,128)(2,1)}, bf16[4,256,1024]{1,2,0:T(8,128)(2,1)}, u32[]{:S(2)}, u32[]{:S(2)}) %collective-permute-start.2) | collective-permute-done | bytes 2097184 | tf_op jit(solution)/shard_map/ppermute | solution.py:22
  385.0 1.9 broadcast_select_fusion.1
  386.9 0.0 copy-start.1
  386.9 2.3 pad_maximum_fusion
  389.2 0.0 copy-done.1
  389.2 48.7 %fusion.9 = f32[4096,8192]{1,0:T(8,128)} fusion(bf16[256,8192]{0,1:T(8,128)(2,1)} %bitcast.17, bf16[256,4096]{1,0:T(8,128)(2,1)S(1)} %copy-done.1, bf16[256,4096]{1,0:T(8,128)(2,1)} %param.5), kind=kOutput, calls=%fused_computation.27 | convolution fusion | flops 17188257792 | bytes 142606336 | tf_op jit(solution)/shard_map/dot_general | solution.py:66
  437.9 0.0 reduce-scatter.5.cloned.1.call-update
  438.0 41.0 %multiply_convert_fusion = (bf16[256,4096]{1,0:T(8,128)(2,1)}, bf16[256,4096]{1,0:T(8,128)(2,1)}) fusion(bf16[256,4096]{1,0:T(8,128)(2,1)} %param.5, bf16[256,4096]{1,0:T(8,128)(2,1)S(1)} %copy-done.1, bf16[256,8192]{0,1:T(8,128)(2,1)} %bitcast.18, bf16[4096,8192]{1,0:T(8,128)(2,1)} %all-gather.2.cloned.1.call-done), kind=kOutput, calls=%fused_computation.16 | convolution fusion | flops 17195597824 | bytes 79691776 | tf_op jit(solution)/shard_map/dot_general | solution.py:60
  479.0 0.0 reduce-scatter.3.cloned.1.call-done
  479.0 1.5 convert_bitcast_fusion
  480.5 1.0 copy.11
  481.5 115.1 %reduce-scatter.5.cloned.1.call-done = f32[4096,4096]{1,0:T(8,128)} async-done(((f32[4096,8192]{1,0:T(8,128)}), f32[4096,4096]{1,0:T(8,128)}) %reduce-scatter.5.cloned.1.call-update) | async-done | bytes 67108880 | tf_op jit(solution)/shard_map/reduce_scatter | solution.py:69
  596.6 32.4 %convert_element_type.43 = bf16[4096,4096]{1,0:T(8,128)(2,1)} convert(f32[4096,4096]{1,0:T(8,128)} %reduce-scatter.5.cloned.1.call-done) | non-fusion elementwise | flops 16777216 | bytes 100663296 | tf_op jit(solution)/shard_map/convert_element_type | solution.py:69
Async XLA Ops:
  7.2 123.2 %all-gather.2.cloned.1.call-start = ((), (), s32[]{:S(2)}) async-start(), calls=%async_computation.2 | async-start | bytes 100663296 | tf_op jit(solution)/shard_map/all_gather | solution.py:44
  32.3 98.0 %copy-start = (bf16[256,4096]{1,0:T(8,128)(2,1)S(1)}, bf16[256,4096]{1,0:T(8,128)(2,1)}, u32[]{:S(2)}) copy-start(bf16[256,4096]{1,0:T(8,128)(2,1)} %param.6) | copy-start | bytes 6291460
  32.4 446.6 %reduce-scatter.3.cloned.1.call-start = ((), (), s32[]{:S(2)}) async-start(), calls=%async_computation.3 | async-start | bytes 9437184 | tf_op jit(solution)/shard_map/reduce_scatter | solution.py:50
  160.7 1.0 copy-start.2
  160.7 435.9 %reduce-scatter.5.cloned.1.call-start = ((), (), s32[]{:S(2)}) async-start(), calls=%async_computation.4 | async-start | bytes 201326592 | tf_op jit(solution)/shard_map/reduce_scatter | solution.py:69
  162.0 20.3 %collective-permute-start = (bf16[1,256,1024]{1,2,0:T(8,128)(2,1)S(1)}, bf16[1,256,1024]{1,2,0:T(8,128)(2,1)S(1)}, u32[]{:S(2)}, u32[]{:S(2)}) collective-permute-start(bf16[1,256,1024]{1,2,0:T(8,128)(2,1)S(1)} %bitcast.19), channel_id=1, source_target_pairs={{0,2},{2,0},{4,6},{6,4},{8,10},{10,8},{12,14},{14,12},{1,3},{3,1},... | collective-permute-start | bytes 1572872 | tf_op jit(solution)/shard_map/ppermute | solution.py:22
  182.4 73.4 %collective-permute-start.1 = (bf16[2,256,1024]{1,2,0:T(8,128)(2,1)S(1)}, bf16[2,256,1024]{1,2,0:T(8,128)(2,1)}, u32[]{:S(2)}, u32[]{:S(2)}) collective-permute-start(bf16[2,256,1024]{1,2,0:T(8,128)(2,1)S(1)} %pad_maximum_fusion.2), channel_id=1, source_target_pairs={{0,4},{2,6},{4,0},{6,2},{8,12},{10,14},{12,8},{14,10},{1,5},{3,7},... | collective-permute-start | bytes 3145736 | tf_op jit(solution)/shard_map/ppermute | solution.py:22
  258.7 126.3 %collective-permute-start.2 = (bf16[4,256,1024]{1,2,0:T(8,128)(2,1)}, bf16[4,256,1024]{1,2,0:T(8,128)(2,1)}, u32[]{:S(2)}, u32[]{:S(2)}) collective-permute-start(bf16[4,256,1024]{1,2,0:T(8,128)(2,1)} %pad_maximum_fusion.1), channel_id=1, source_target_pairs={{0,8},{2,10},{4,12},{6,14},{8,0},{10,2},{12,4},{14,6},{1,9},{3,11}... | collective-permute-start | bytes 6291464 | tf_op jit(solution)/shard_map/ppermute | solution.py:22
  386.9 2.3 copy-start.1
Sparse Core Ops, SparseCore 0:
  32.5 97.7 all-gather.1
  160.9 199.2 reduce-scatter.2
  438.1 158.5 reduce-scatter.4
